TPU v7x, 32 devices: a whole 2x2x4 slice. The times are simulated.
32 devices in a mesh: dp: 4 (over x, core), row: 2 (over y), col: 4 (over z).
Axes of the slice: x: 2, y: 2, z: 4, core: 2. Of those that a mesh axis runs over, the one named last changes fastest.
Arguments:
- tokens: bfloat16 [4096, 2048], P(('dp', 'row'), 'col'), may hold values from -6 to 6
- parent: int32 [4, 4], P('dp'), may hold values from -1 to 1, as said below
- depth: int32 [4, 4], P('dp'), may hold values from 0 to 2, as said below
- w_qkv: float32 [2048, 6144], P('row', 'col'), may hold values from -0.125 to 0.125
- b_qkv: float32 [6144], P('col'), may hold values from -3 to 3
- w_out: float32 [2048, 2048], P('col', 'row'), may hold values from -0.75 to 0.75
- w_up: float32 [2048, 8192], P('row', 'col'), may hold values from -0.125 to 0.125
- b_up: float32 [8192], P('col'), may hold values from -3 to 3
- w_down: float32 [8192, 2048], P('col', 'row'), may hold values from -0.0625 to 0.0625
- b_res: float32 [2048], P('col'), may hold values from -3 to 3
- ln_gain: float32 [2048], replicated, may hold values from 0.5 to 1.5
- ln_bias: float32 [2048], replicated, may hold values from -2 to 2
- cotangent: bfloat16 [4096, 2048], P(('dp', 'row'), 'col'), may hold values from -6 to 6
Outputs:
- output: bfloat16 [4096, 2048], P(('dp', 'row'), 'col')
- tokens_grad: float32 [4096, 2048], P(('dp', 'row'), 'col')
- w_qkv_grad: float32 [2048, 6144], P('row', 'col')
- b_qkv_grad: float32 [6144], P('col')
- w_out_grad: float32 [2048, 2048], P('col', 'row')
- w_up_grad: float32 [2048, 8192], P('row', 'col')
- b_up_grad: float32 [8192], P('col')
- w_down_grad: float32 [8192, 2048], P('col', 'row')
- b_res_grad: float32 [2048], P('col')
- ln_gain_grad: float32 [2048], replicated
- ln_bias_grad: float32 [2048], replicated
Inputs may be any that keep to these rules, and one draw needn't show every extreme that they name: In every tree segments 0 to 1 form a trunk: segment 0 has parent -1 and each other trunk segment j has parent j - 1. Every later segment has a trunk segment as parent, and the last segment's parent is trunk segment 4 // 2 - 1. Segment 0 has depth 0 and every other segment one more than its parent.
All inputs are finite; a program needn't handle non-finite values.
Results may differ from a plain program's by a relative error of at most 0.018.
Values may be sent and summed in bfloat16 or wider, within the bound.
No kernel may reach another device: no remote copies, remote signals or barrier semaphores. Data moves between devices by JAX's collectives and lax.ppermute only.
A program may use at most 256 MiB of HBM per device.

v0:
```python
import functools
import math
import jax
import jax.numpy as jnp
from jax import lax
from jax.sharding import PartitionSpec as P

HD = 64
ROT = 32
SEG = 256
norm_epsilon = 1e-05
masked_fill = -1e30
rotary_base = 10000.0


def precise_dot(left, right):
    return jnp.dot(left, right, precision=lax.Precision.HIGHEST, preferred_element_type=jnp.float32)


def ancestry(parent_row):
    seg_count = parent_row.shape[0]
    labels = jnp.arange(seg_count, dtype=jnp.int32)
    identity = jnp.eye(seg_count, dtype=jnp.float32)
    parent_hot = (parent_row[:, None] == labels[None, :]).astype(jnp.float32)

    def extend(rounds, reachable):
        return jnp.minimum(identity + precise_dot(parent_hot, reachable), 1.0)

    return lax.fori_loop(0, seg_count, extend, identity)


def rotate(values, cosines, sines):
    half_rot = ROT // 2
    former = values[..., :half_rot]
    latter = values[..., half_rot:ROT]
    return jnp.concatenate(
        [former * cosines - latter * sines, latter * cosines + former * sines, values[..., ROT:]],
        axis=-1,
    )


def angles_of(positions):
    frequency = jnp.exp(
        -math.log(rotary_base) * 2.0 * jnp.arange(ROT // 2, dtype=jnp.float32) / ROT
    )
    phase_angle = positions[:, None] * frequency[None, :]
    return (jnp.cos(phase_angle)[:, None, :], jnp.sin(phase_angle)[:, None, :])


def reorder_rows(gradient, row_count, dp_count):
    leading = gradient.shape[0]
    blocked = gradient.reshape(
        row_count, dp_count, leading // (row_count * dp_count), gradient.shape[1]
    )
    return jnp.transpose(blocked, (1, 0, 2, 3)).reshape(leading, gradient.shape[1])


def reorder_cols(gradient, row_count, dp_count):
    trailing = gradient.shape[1]
    blocked = gradient.reshape(
        gradient.shape[0], row_count, dp_count, trailing // (row_count * dp_count)
    )
    return jnp.transpose(blocked, (0, 2, 1, 3)).reshape(gradient.shape[0], trailing)


def per_device(
    tokens,
    parent,
    depth,
    w_qkv,
    b_qkv,
    w_out,
    w_up,
    b_up,
    w_down,
    b_res,
    ln_gain,
    ln_bias,
    cotangent,
):
    tok_rows = tokens.shape[0]
    col_width = tokens.shape[1]
    row_count = lax.axis_size("row")
    dp_count = lax.axis_size("dp")
    row_start = lax.axis_index("row") * tok_rows
    local_heads = w_out.shape[0] // HD
    seg_count = parent.shape[1]
    labels = jnp.arange(seg_count, dtype=jnp.int32)
    reachable = ancestry(parent[0])
    query_index = row_start + jnp.arange(tok_rows, dtype=jnp.int32)
    query_seg = query_index // SEG
    query_hot = (query_seg[:, None] == labels[None, :]).astype(jnp.float32)
    query_reach = precise_dot(query_hot, reachable)
    levels = precise_dot(query_hot, depth[0].astype(jnp.float32)[:, None])[:, 0]
    positions = levels * SEG + (query_index % SEG).astype(jnp.float32)
    cosines, sines = angles_of(positions)
    score_scale = HD ** (-0.5)

    def permit(key_len):
        key_index = jnp.arange(key_len, dtype=jnp.int32)
        key_seg = key_index // SEG
        key_hot = (key_seg[:, None] == labels[None, :]).astype(jnp.float32)
        linked = precise_dot(query_reach, key_hot.T) > 0.5
        return linked & (
            (query_seg[:, None] != key_seg[None, :]) | (query_index[:, None] >= key_index[None, :])
        )

    whole = lax.all_gather(tokens, "col", axis=1, tiled=True).astype(jnp.float32)
    centred = whole - jnp.mean(whole, axis=1, keepdims=True)
    inv_scale = lax.rsqrt(jnp.mean(centred * centred, axis=1, keepdims=True) + norm_epsilon)
    normal = centred * inv_scale
    normed = (normal * ln_gain + ln_bias).astype(jnp.bfloat16)
    qkv_full, up_full, out_full, down_full = (
        lax.all_gather(w_qkv.astype(jnp.bfloat16), "row", axis=0, tiled=True),
        lax.all_gather(w_up.astype(jnp.bfloat16), "row", axis=0, tiled=True),
        lax.all_gather(w_out.astype(jnp.bfloat16), "row", axis=1, tiled=True),
        lax.all_gather(w_down.astype(jnp.bfloat16), "row", axis=1, tiled=True),
    )
    mixed = (jnp.dot(normed, qkv_full, preferred_element_type=jnp.float32) + b_qkv).reshape(
        tok_rows, local_heads, 3, HD
    )

    def rotate_pair(query_pre, key_pre):
        return (rotate(query_pre, cosines, sines), rotate(key_pre, cosines, sines))

    rotated, rotate_back = jax.vjp(rotate_pair, mixed[:, :, 0], mixed[:, :, 1])
    queries = rotated[0].astype(jnp.bfloat16)
    key_rows = rotated[1].astype(jnp.bfloat16)
    value_rows = mixed[:, :, 2].astype(jnp.bfloat16)
    key_flat = key_rows.reshape(tok_rows, local_heads * HD)
    value_flat = value_rows.reshape(tok_rows, local_heads * HD)

    def scores_for(key_part):
        raw_scores = (
            jnp.einsum("qhe,khe->hqk", queries, key_part, preferred_element_type=jnp.float32)
            * score_scale
        )
        allowed = permit(key_part.shape[0])
        return (jnp.where(allowed[None], raw_scores, masked_fill), allowed)

    pieces = (
        lax.all_gather(key_flat, "row", axis=0, tiled=True),
        lax.all_gather(value_flat, "row", axis=0, tiled=True),
    )
    running_top = jnp.full((local_heads, tok_rows), masked_fill, jnp.float32)
    key_len = pieces[0].shape[0]
    key_part = pieces[0].reshape(key_len, local_heads, HD)
    value_part = pieces[1].reshape(key_len, local_heads, HD)
    scores, allowed = scores_for(key_part)
    new_top = jnp.maximum(running_top, jnp.max(scores, axis=2))
    exponent = jnp.where(allowed[None], jnp.exp(scores - new_top[:, :, None]), 0.0)
    running_sum = jnp.sum(exponent, axis=2)
    weighted = jnp.einsum(
        "hqk,khe->hqe",
        exponent.astype(jnp.bfloat16),
        value_part,
        preferred_element_type=jnp.float32,
    )
    running_top, running_sum, weighted = (new_top, running_sum, weighted)
    log_total = running_top + jnp.log(running_sum)
    attn_exact = weighted / running_sum[:, :, None]
    attended = (
        jnp.transpose(attn_exact, (1, 0, 2))
        .reshape(tok_rows, local_heads * HD)
        .astype(jnp.bfloat16)
    )
    hidden_up = jnp.dot(normed, up_full, preferred_element_type=jnp.float32) + b_up
    activated, gelu_back = jax.vjp(functools.partial(jax.nn.gelu, approximate=True), hidden_up)
    activated = activated.astype(jnp.bfloat16)
    branch_terms = jnp.dot(attended, out_full, preferred_element_type=jnp.float32) + jnp.dot(
        activated, down_full, preferred_element_type=jnp.float32
    )
    branch = lax.psum_scatter(
        branch_terms.astype(jnp.bfloat16), "col", scatter_dimension=1, tiled=True
    ).astype(jnp.float32)
    output = (tokens.astype(jnp.float32) + branch + b_res).astype(jnp.bfloat16)
    grad_full = lax.all_gather(cotangent, "col", axis=1, tiled=True)
    res_bias_grad = jnp.sum(cotangent.astype(jnp.float32), axis=0)
    down_grad = jnp.einsum("tf,td->fd", activated, grad_full, preferred_element_type=jnp.float32)
    out_grad = jnp.einsum("te,td->ed", attended, grad_full, preferred_element_type=jnp.float32)
    act_grad = jnp.einsum("td,fd->tf", grad_full, down_full, preferred_element_type=jnp.float32)
    up_grad = gelu_back(act_grad)[0].astype(jnp.bfloat16)
    attn_grad = jnp.einsum(
        "td,ed->te", grad_full, out_full, preferred_element_type=jnp.float32
    ).astype(jnp.bfloat16)
    up_bias_grad = jnp.sum(up_grad.astype(jnp.float32), axis=0)
    up_weight_grad = jnp.einsum("td,tf->df", normed, up_grad, preferred_element_type=jnp.float32)
    out_heads = attn_grad.reshape(tok_rows, local_heads, HD)
    delta_sum = jnp.einsum("qhe,hqe->hq", out_heads.astype(jnp.float32), attn_exact)
    pieces = (
        lax.all_gather(key_flat, "row", axis=0, tiled=True),
        lax.all_gather(value_flat, "row", axis=0, tiled=True),
    )
    key_len = pieces[0].shape[0]
    key_part = pieces[0].reshape(key_len, local_heads, HD)
    value_part = pieces[1].reshape(key_len, local_heads, HD)
    scores, allowed = scores_for(key_part)
    softmaxed = jnp.where(allowed[None], jnp.exp(scores - log_total[:, :, None]), 0.0)
    prob_grad = jnp.einsum(
        "qhe,khe->hqk", out_heads, value_part, preferred_element_type=jnp.float32
    )
    score_grad = (softmaxed * (prob_grad - delta_sum[:, :, None])).astype(jnp.bfloat16)
    query_grad = (
        jnp.einsum("hqk,khe->qhe", score_grad, key_part, preferred_element_type=jnp.float32)
        * score_scale
    )
    key_grad = (
        jnp.einsum("hqk,qhe->khe", score_grad, queries, preferred_element_type=jnp.float32)
        * score_scale
    )
    value_grad = jnp.einsum(
        "hqk,qhe->khe",
        softmaxed.astype(jnp.bfloat16),
        out_heads,
        preferred_element_type=jnp.float32,
    )
    stacked = jnp.stack([key_grad, value_grad], axis=1).reshape(key_len, 2 * local_heads * HD)
    pair_grad = stacked
    query_grad, pair_grad = (query_grad, pair_grad)
    own_pairs = (
        lax.psum_scatter(pair_grad.astype(jnp.bfloat16), "row", scatter_dimension=0, tiled=True)
        .astype(jnp.float32)
        .reshape(tok_rows, 2, local_heads, HD)
    )
    query_pre, key_pre = rotate_back((query_grad, own_pairs[:, 0]))
    mixed_grad = (
        jnp.stack([query_pre, key_pre, own_pairs[:, 1]], axis=2)
        .reshape(tok_rows, 3 * local_heads * HD)
        .astype(jnp.bfloat16)
    )
    qkv_bias_grad = jnp.sum(mixed_grad.astype(jnp.float32), axis=0)
    qkv_weight_grad = jnp.einsum(
        "td,tc->dc", normed, mixed_grad, preferred_element_type=jnp.float32
    )
    norm_part = jnp.einsum(
        "tc,dc->td", mixed_grad, qkv_full, preferred_element_type=jnp.float32
    ) + jnp.einsum("tf,df->td", up_grad, up_full, preferred_element_type=jnp.float32)
    norm_grad = lax.psum(norm_part.astype(jnp.bfloat16), "col").astype(jnp.float32)
    gain_grad = jnp.sum(norm_grad * normal, axis=0)
    shift_grad = jnp.sum(norm_grad, axis=0)
    scaled = norm_grad * ln_gain
    mean_scaled = jnp.mean(scaled, axis=1, keepdims=True)
    mean_mixed = jnp.mean(scaled * normal, axis=1, keepdims=True)
    col_start = lax.axis_index("col") * col_width
    scaled_share = lax.dynamic_slice_in_dim(scaled, col_start, col_width, 1)
    normal_share = lax.dynamic_slice_in_dim(normal, col_start, col_width, 1)
    tokens_grad = inv_scale * (
        scaled_share - mean_scaled - normal_share * mean_mixed
    ) + cotangent.astype(jnp.float32)
    qkv_bias_grad, up_bias_grad, res_bias_grad, gain_grad, shift_grad = (
        lax.psum(qkv_bias_grad.astype(jnp.bfloat16), ("dp", "row")).astype(jnp.float32),
        lax.psum(up_bias_grad.astype(jnp.bfloat16), ("dp", "row")).astype(jnp.float32),
        lax.psum(res_bias_grad.astype(jnp.bfloat16), ("dp", "row")).astype(jnp.float32),
        lax.psum(gain_grad.astype(jnp.bfloat16), ("dp", "row")).astype(jnp.float32),
        lax.psum(shift_grad.astype(jnp.bfloat16), ("dp", "row")).astype(jnp.float32),
    )
    pieces_now = (
        lax.psum_scatter(
            reorder_rows(qkv_weight_grad, row_count, dp_count).astype(jnp.bfloat16),
            ("dp", "row"),
            scatter_dimension=0,
            tiled=True,
        ).astype(jnp.float32),
        lax.psum_scatter(
            reorder_rows(up_weight_grad, row_count, dp_count).astype(jnp.bfloat16),
            ("dp", "row"),
            scatter_dimension=0,
            tiled=True,
        ).astype(jnp.float32),
        lax.psum_scatter(
            reorder_cols(out_grad, row_count, dp_count).astype(jnp.bfloat16),
            ("dp", "row"),
            scatter_dimension=1,
            tiled=True,
        ).astype(jnp.float32),
        lax.psum_scatter(
            reorder_cols(down_grad, row_count, dp_count).astype(jnp.bfloat16),
            ("dp", "row"),
            scatter_dimension=1,
            tiled=True,
        ).astype(jnp.float32),
    )
    qkv_weight_grad, up_weight_grad, out_grad, down_grad = (
        lax.all_gather(pieces_now[0].astype(jnp.bfloat16), "dp", axis=0, tiled=True).astype(
            jnp.float32
        ),
        lax.all_gather(pieces_now[1].astype(jnp.bfloat16), "dp", axis=0, tiled=True).astype(
            jnp.float32
        ),
        lax.all_gather(pieces_now[2].astype(jnp.bfloat16), "dp", axis=1, tiled=True).astype(
            jnp.float32
        ),
        lax.all_gather(pieces_now[3].astype(jnp.bfloat16), "dp", axis=1, tiled=True).astype(
            jnp.float32
        ),
    )
    return (
        output,
        tokens_grad,
        qkv_weight_grad,
        qkv_bias_grad,
        out_grad,
        up_weight_grad,
        up_bias_grad,
        down_grad,
        res_bias_grad,
        gain_grad,
        shift_grad,
    )


def solution(mesh):
    return jax.shard_map(
        per_device,
        mesh=mesh,
        in_specs=(
            P(("dp", "row"), "col"),
            P("dp", None),
            P("dp", None),
            P("row", "col"),
            P("col"),
            P("col", "row"),
            P("row", "col"),
            P("col"),
            P("col", "row"),
            P("col"),
            P(),
            P(),
            P(("dp", "row"), "col"),
        ),
        out_specs=(
            P(("dp", "row"), "col"),
            P(("dp", "row"), "col"),
            P("row", "col"),
            P("col"),
            P("col", "row"),
            P("row", "col"),
            P("col"),
            P("col", "row"),
            P("col"),
            P(),
            P(),
        ),
        check_vma=False,
    )
```

profile of v0, /device:TPU:0, one launch (start us, length us, event | category | flops | bytes accessed | tf_op | source)
XLA Modules:
  0.0 1054.9 jit_solution(18216092555689512656)
XLA Ops:
  16.1 41.9 %all-gather.13.cloned.1.call-done = bf16[512,2048]{1,0:T(8,128)(2,1)} async-done(((bf16[512,512]{1,0:T(8,128)(2,1)}), bf16[512,2048]{1,0:T(8,128)(2,1)}) %all-gather.13.cloned.1.call-update) | async-done | bytes 2097168 | tf_op jit(solution)/shard_map/all_gather | solution.py:108
  62.4 76.9 %all-gather.15.cloned.1.call-done = bf16[2048,1536]{1,0:T(8,128)(2,1)} async-done(((bf16[1024,1536]{1,0:T(8,128)(2,1)}), bf16[2048,1536]{1,0:T(8,128)(2,1)}) %all-gather.15.cloned.1.call-update) | async-done | bytes 6291472 | tf_op jit(solution)/shard_map/all_gather | solution.py:114
  174.5 47.1 %all-gather.27.cloned.1.call-done = bf16[512,2048]{1,0:T(8,128)(2,1)} async-done(((bf16[512,512]{1,0:T(8,128)(2,1)}), bf16[512,2048]{1,0:T(8,128)(2,1)}) %all-gather.27.cloned.1.call-update) | async-done | bytes 2097168 | tf_op jit(solution)/shard_map/all_gather | solution.py:177
  227.0 16.7 %all-gather.17.cloned.1.call-done = bf16[1024,512]{0,1:T(8,128)(2,1)} async-done(((bf16[512,512]{0,1:T(8,128)(2,1)}), bf16[1024,512]{0,1:T(8,128)(2,1)}) %all-gather.17.cloned.1.call-update) | async-done | bytes 1048592 | tf_op jit(solution)/shard_map/all_gather | solution.py:142
  254.9 12.1 %all-gather.19.cloned.1.call-done = bf16[1024,512]{0,1:T(8,128)(2,1)} async-done(((bf16[512,512]{0,1:T(8,128)(2,1)}), bf16[1024,512]{0,1:T(8,128)(2,1)}) %all-gather.19.cloned.1.call-update) | async-done | bytes 1048592 | tf_op jit(solution)/shard_map/all_gather | solution.py:143
  280.0 9.9 multiply_convert_fusion
  307.6 65.6 %all-gather.23.cloned.1.call-done = bf16[2048,2048]{1,0:T(8,128)(2,1)} async-done(((bf16[1024,2048]{1,0:T(8,128)(2,1)}), bf16[2048,2048]{1,0:T(8,128)(2,1)}) %all-gather.23.cloned.1.call-update) | async-done | bytes 8388624 | tf_op jit(solution)/shard_map/all_gather | solution.py:115
  373.2 9.9 fusion.64
  383.0 96.3 %all-gather.25.cloned.1.call-done = bf16[2048,2048]{1,0:T(8,128)(2,1)} async-done(((bf16[2048,1024]{1,0:T(8,128)(2,1)}), bf16[2048,2048]{1,0:T(8,128)(2,1)}) %all-gather.25.cloned.1.call-update) | async-done | bytes 8388624 | tf_op jit(solution)/shard_map/all_gather | solution.py:117
  479.3 13.4 %fusion.65 = (bf16[2048]{0:T(1024)(128)(2,1)S(1)}, bf16[512,2048]{1,0:T(8,128)(2,1)}) fusion(f32[512,2048]{1,0:T(8,128)} %fusion.64, f32[2048]{0:T(1024)S(1)} %copy-done.29, bf16[512,2048]{1,0:T(8,128)(2,1)} %all-gather.27.cloned.1.call-done, bf16[2048,2048]{1,0:T(8,128)(2,1)} %all-gather.25.cloned.1.call-done), kind=kOutput, calls=%fused_computation.132 | convolution fusion | flops 4318033920 | bytes 16789504 | tf_op jit(solution)/shard_map/td,fd->tf/dot_general | solution.py:181
  492.7 21.3 %reduce-scatter.9.cloned.1.call-done = bf16[512,1024]{0,1:T(8,128)(2,1)} async-done(((bf16[1024,1024]{0,1:T(8,128)(2,1)}), bf16[512,1024]{0,1:T(8,128)(2,1)}) %reduce-scatter.9.cloned.1.call-update) | async-done | bytes 1048592 | tf_op jit(solution)/shard_map/reduce_scatter | solution.py:221
  556.4 11.0 %convolution_convert_fusion = bf16[2048,2048]{0,1:T(8,128)(2,1)} fusion(bf16[512,2048]{1,0:T(8,128)(2,1)} %all-gather.27.cloned.1.call-done, f32[512,2048]{1,0:T(8,128)} %fusion.64, f32[2048]{0:T(1024)S(1)} %copy-done.29), kind=kOutput, calls=%fused_computation.21 | convolution fusion | flops 4309647360 | bytes 14688256 | tf_op jit(solution)/shard_map/tf,td->fd/dot_general | solution.py:179
  567.4 21.7 %copy.57 = bf16[2048,4,2,256]{3,2,1,0:T(2,128)(2,1)} copy(bf16[2048,4,2,256]{0,3,1,2:T(8,128)(2,1)} %bitcast.110) | data formatting | bytes 16777216 | tf_op jit(solution)/shard_map/convert_element_type | solution.py:277
  589.2 14.4 %convert_element_type.255 = bf16[2048,2048]{1,0:T(8,128)(2,1)} reshape(bf16[2048,4,2,256]{3,2,1,0:T(2,128)(2,1)} %copy.57) | data formatting | bytes 16777216 | tf_op jit(solution)/shard_map/convert_element_type | solution.py:277
  603.7 13.1 %all-reduce.9.cloned.1.call-done = bf16[512,2048]{1,0:T(8,128)(2,1)} async-done(((bf16[512,2048]{1,0:T(8,128)(2,1)}), bf16[512,2048]{1,0:T(8,128)(2,1)}) %all-reduce.9.cloned.1.call-update) | async-done | bytes 2097168 | tf_op jit(solution)/shard_map/psum | solution.py:238
  634.6 25.6 %reduce-scatter.13.cloned.1.call-done = bf16[512,256]{0,1:T(8,128)(2,1)} async-done(((bf16[512,2048]{0,1:T(8,128)(2,1)}), bf16[512,256]{0,1:T(8,128)(2,1)}) %reduce-scatter.13.cloned.1.call-update) | async-done | bytes 262160 | tf_op jit(solution)/shard_map/reduce_scatter | solution.py:270
  672.4 63.2 %reduce-scatter.15.cloned.1.call-done = bf16[256,2048]{1,0:T(8,128)(2,1)} async-done(((bf16[2048,2048]{1,0:T(8,128)(2,1)}), bf16[256,2048]{1,0:T(8,128)(2,1)}) %reduce-scatter.15.cloned.1.call-update) | async-done | bytes 1048592 | tf_op jit(solution)/shard_map/reduce_scatter | solution.py:264
  735.7 75.3 %reduce-scatter.17.cloned.1.call-done = bf16[2048,256]{1,0:T(8,128)(2,1)} async-done(((bf16[2048,2048]{1,0:T(8,128)(2,1)}), bf16[2048,256]{1,0:T(8,128)(2,1)}) %reduce-scatter.17.cloned.1.call-update) | async-done | bytes 1048592 | tf_op jit(solution)/shard_map/reduce_scatter | solution.py:276
  811.1 65.6 %reduce-scatter.11.cloned.1.call-done = bf16[256,1536]{1,0:T(8,128)(2,1)} async-done(((bf16[2048,1536]{1,0:T(8,128)(2,1)}), bf16[256,1536]{1,0:T(8,128)(2,1)}) %reduce-scatter.11.cloned.1.call-update) | async-done | bytes 786448 | tf_op jit(solution)/shard_map/reduce_scatter | solution.py:258
  876.9 17.9 %all-gather.31.cloned.1.call-done = bf16[512,1024]{0,1:T(8,128)(2,1)} async-done(((bf16[512,256]{0,1:T(8,128)(2,1)}), bf16[512,1024]{0,1:T(8,128)(2,1)}) %all-gather.31.cloned.1.call-update) | async-done | bytes 1048592 | tf_op jit(solution)/shard_map/all_gather | solution.py:290
  897.3 43.2 %reduce-scatter.7.cloned.1.call-done = bf16[512,512]{1,0:T(8,128)(2,1)} async-done(((bf16[512,2048]{1,0:T(8,128)(2,1)}), bf16[512,512]{1,0:T(8,128)(2,1)}) %reduce-scatter.7.cloned.1.call-update) | async-done | bytes 524304 | tf_op jit(solution)/shard_map/reduce_scatter | solution.py:173
  942.9 25.2 %all-reduce.6 = (bf16[1536]{0:T(1024)(128)(2,1)S(1)}, bf16[2048]{0:T(1024)(128)(2,1)S(1)}, bf16[512]{0:T(512)(128)(2,1)S(1)}, bf16[2048]{0:T(1024)(128)(2,1)S(1)}, bf16[2048]{0:T(1024)(128)(2,1)S(1)}) all-reduce(bf16[1536]{0:T(1024)(128)(2,1)S(1)} %reduce_sum.110, ...), channel_id=1, replica_groups=mesh['dp'=4,'row'=2,'col'=4] {'dp','row'}, use_global_device_ids=true, to_apply=%region_13.14 | all-reduce | flops 8192 | bytes 32768 | tf_op jit(solution)/shard_map/psum | solution.py:251
  982.5 29.9 %all-gather.35.cloned.1.call-done = bf16[2048,1024]{1,0:T(8,128)(2,1)} async-done(((bf16[2048,256]{1,0:T(8,128)(2,1)}), bf16[2048,1024]{1,0:T(8,128)(2,1)}) %all-gather.35.cloned.1.call-update) | async-done | bytes 4194320 | tf_op jit(solution)/shard_map/all_gather | solution.py:293
  1019.0 23.5 %all-gather.29.cloned.1.call-done = bf16[1024,1536]{1,0:T(8,128)(2,1)} async-done(((bf16[256,1536]{1,0:T(8,128)(2,1)}), bf16[1024,1536]{1,0:T(8,128)(2,1)}) %all-gather.29.cloned.1.call-update) | async-done | bytes 3145744 | tf_op jit(solution)/shard_map/all_gather | solution.py:284
  (199 shorter events, 200.0 us)
Async XLA Ops:
  7.2 50.8 %all-gather.13.cloned.1.call-start = ((), (), s32[]{:S(2)}) async-start(), calls=%async_computation.6 | async-start | bytes 2621440 | tf_op jit(solution)/shard_map/all_gather | solution.py:108
  7.9 131.4 %all-gather.15.cloned.1.call-start = ((), (), s32[]{:S(2)}) async-start(), calls=%async_computation.7 | async-start | bytes 9437184 | tf_op jit(solution)/shard_map/all_gather | solution.py:114
  13.0 161.5 %all-gather.21.cloned.1.call-start = ((), (), s32[]{:S(2)}) async-start(), calls=%async_computation.10 | async-start | bytes 3145728 | tf_op jit(solution)/shard_map/all_gather | solution.py:116
  14.2 207.4 %all-gather.27.cloned.1.call-start = ((), (), s32[]{:S(2)}) async-start(), calls=%async_computation.14 | async-start | bytes 2621440 | tf_op jit(solution)/shard_map/all_gather | solution.py:177
  14.8 228.9 %all-gather.17.cloned.1.call-start = ((), (), s32[]{:S(2)}) async-start(), calls=%async_computation.8 | async-start | bytes 1572864 | tf_op jit(solution)/shard_map/all_gather | solution.py:142
  152.2 114.9 %all-gather.19.cloned.1.call-start = ((), (), s32[]{:S(2)}) async-start(), calls=%async_computation.9 | async-start | bytes 1572864 | tf_op jit(solution)/shard_map/all_gather | solution.py:143
  153.1 220.1 %all-gather.23.cloned.1.call-start = ((), (), s32[]{:S(2)}) async-start(), calls=%async_computation.11 | async-start | bytes 12582912 | tf_op jit(solution)/shard_map/all_gather | solution.py:115
  159.2 320.1 %all-gather.25.cloned.1.call-start = ((), (), s32[]{:S(2)}) async-start(), calls=%async_computation.12 | async-start | bytes 12582912 | tf_op jit(solution)/shard_map/all_gather | solution.py:117
  165.4 348.7 %reduce-scatter.9.cloned.1.call-start = ((), (), s32[]{:S(2)}) async-start(), calls=%async_computation.15 | async-start | bytes 3145728 | tf_op jit(solution)/shard_map/reduce_scatter | solution.py:221
  300.2 316.6 %all-reduce.9.cloned.1.call-start = ((), (), s32[]{:S(2)}) async-start(), calls=%async_computation.16 | async-start | bytes 4194304 | tf_op jit(solution)/shard_map/psum | solution.py:238
  307.6 171.7 %copy-start.29 = (f32[2048]{0:T(1024)S(1)}, f32[2048]{0:T(1024)}, u32[]{:S(2)}) copy-start(f32[2048]{0:T(1024)} %param.22) | copy-start | bytes 24580
  530.4 129.8 %reduce-scatter.13.cloned.1.call-start = ((), (), s32[]{:S(2)}) async-start(), calls=%async_computation.19 | async-start | bytes 2359296 | tf_op jit(solution)/shard_map/reduce_scatter | solution.py:270
  539.0 196.6 %reduce-scatter.15.cloned.1.call-start = ((), (), s32[]{:S(2)}) async-start(), calls=%async_computation.21 | async-start | bytes 9437184 | tf_op jit(solution)/shard_map/reduce_scatter | solution.py:264
  556.4 254.6 %reduce-scatter.17.cloned.1.call-start = ((), (), s32[]{:S(2)}) async-start(), calls=%async_computation.23 | async-start | bytes 9437184 | tf_op jit(solution)/shard_map/reduce_scatter | solution.py:276
  603.6 273.0 %reduce-scatter.11.cloned.1.call-start = ((), (), s32[]{:S(2)}) async-start(), calls=%async_computation.17 | async-start | bytes 7077888 | tf_op jit(solution)/shard_map/reduce_scatter | solution.py:258
  634.5 260.2 %all-gather.31.cloned.1.call-start = ((), (), s32[]{:S(2)}) async-start(), calls=%async_computation.20 | async-start | bytes 1310720 | tf_op jit(solution)/shard_map/all_gather | solution.py:290
  660.2 280.3 %reduce-scatter.7.cloned.1.call-start = ((), (), s32[]{:S(2)}) async-start(), calls=%async_computation.13 | async-start | bytes 2621440 | tf_op jit(solution)/shard_map/reduce_scatter | solution.py:173
  672.3 204.3 %copy-start.5 = (bf16[512,512]{1,0:T(8,128)(2,1)S(1)}, bf16[512,512]{1,0:T(8,128)(2,1)}, u32[]{:S(2)}) copy-start(bf16[512,512]{1,0:T(8,128)(2,1)} %param.27) | copy-start | bytes 1572868
  672.3 268.2 %copy-start.8 = (bf16[512,512]{1,0:T(8,128)(2,1)S(1)}, bf16[512,512]{1,0:T(8,128)(2,1)}, u32[]{:S(2)}) copy-start(bf16[512,512]{1,0:T(8,128)(2,1)} %param.15) | copy-start | bytes 1572868
  672.3 268.2 %copy-start.27 = (f32[512]{0:T(512)S(1)}, f32[512]{0:T(512)}, u32[]{:S(2)}) copy-start(f32[512]{0:T(512)} %param.24) | copy-start | bytes 6148
  672.3 270.2 %copy-start.4 = (bf16[512,2048]{1,0:T(8,128)(2,1)S(1)}, bf16[512,2048]{1,0:T(8,128)(2,1)}, u32[]{:S(2)}) copy-start(bf16[512,2048]{1,0:T(8,128)(2,1)} %all-reduce.9.cloned.1.call-done) | copy-start | bytes 6291460
  672.4 303.5 %all-gather.33.cloned.1.call-start = ((), (), s32[]{:S(2)}) async-start(), calls=%async_computation.22 | async-start | bytes 5242880 | tf_op jit(solution)/shard_map/all_gather | solution.py:287
  735.6 276.7 %all-gather.35.cloned.1.call-start = ((), (), s32[]{:S(2)}) async-start(), calls=%async_computation.24 | async-start | bytes 5242880 | tf_op jit(solution)/shard_map/all_gather | solution.py:293
  811.0 231.4 %all-gather.29.cloned.1.call-start = ((), (), s32[]{:S(2)}) async-start(), calls=%async_computation.18 | async-start | bytes 3932160 | tf_op jit(solution)/shard_map/all_gather | solution.py:284
  (31 other events, 839.1 us)
Sparse Core Ops, SparseCore 0:
  9.6 48.3 all-gather.12
  60.1 79.1 all-gather.14
  141.4 33.0 all-gather.20
  176.0 45.6 all-gather.26
  223.6 20.0 all-gather.16
  245.7 21.2 all-gather.18
  269.1 104.0 all-gather.22
  375.3 103.9 all-gather.24
  482.1 31.8 reduce-scatter.8
  530.5 86.1 all-reduce.8
  620.0 40.1 reduce-scatter.12
  664.1 71.4 reduce-scatter.14
  739.7 71.2 reduce-scatter.16
  814.8 61.7 reduce-scatter.10
  878.0 16.6 all-gather.30
  896.9 43.6 reduce-scatter.6
  942.0 33.8 all-gather.32
  977.2 35.0 all-gather.34
  1013.9 28.4 all-gather.28
where the time goes:
time: 1060 us; the launch traced here: 1050 us
  waiting for transfers between devices  744 us (70%)
  matrix products  128 us (12%)
  local copies, waits for them, and re-layouts  74.6 us (7%)
  other arithmetic  67.1 us (6%)
  blocking collectives  25.2 us (2%)
  between operations  15 us (1%)
    all_gather x1, waiting for transfers between devices, per_device(): lax.all_gather(w_down.astype(jnp.bfloat16), 'row', axis=1, tiled=True)  96.3 us
    all_gather x1, waiting for transfers between devices, per_device(): lax.all_gather(w_qkv.astype(jnp.bfloat16), 'row', axis=0, tiled=True)  76.9 us
    reduce_scatter x1, waiting for transfers between devices, per_device(): lax.psum_scatter(reorder_cols(down_grad, row_count, dp_count).astype(jnp....  75.3 us
    all_gather x1, waiting for transfers between devices, per_device(): lax.all_gather(w_up.astype(jnp.bfloat16), 'row', axis=0, tiled=True)  65.6 us
    reduce_scatter x1, waiting for transfers between devices, per_device(): lax.psum_scatter(reorder_rows(qkv_weight_grad, row_count, dp_count).astyp...  65.6 us
    reduce_scatter x1, waiting for transfers between devices, per_device(): lax.psum_scatter(reorder_rows(up_weight_grad, row_count, dp_count).astype...  63.2 us
    all_gather x1, waiting for transfers between devices, per_device(): grad_full = lax.all_gather(cotangent, 'col', axis=1, tiled=True)  47.1 us
    reduce_scatter x1, waiting for transfers between devices, per_device(): lax.psum_scatter(branch_terms.astype(jnp.bfloat16), 'col', scatter_dimens...  43.2 us
  transfers between devices with their start and end apart: 19, of which 19 were waited for; matrix products, arithmetic and copies ran while one was open for 23% of the time, Pallas kernels for 0%

commit v1 on v0

--- a/solution.py
+++ b/solution.py
@@ -248,7 +248,9 @@
         scaled_share - mean_scaled - normal_share * mean_mixed
     ) + cotangent.astype(jnp.float32)
     qkv_bias_grad, up_bias_grad, res_bias_grad, gain_grad, shift_grad = (
-        lax.psum(qkv_bias_grad.astype(jnp.bfloat16), ("dp", "row")).astype(jnp.float32),
+        jnp.sum(lax.all_gather(qkv_bias_grad.astype(jnp.bfloat16), ("dp", "row")), axis=0).astype(
+            jnp.float32
+        ),
         lax.psum(up_bias_grad.astype(jnp.bfloat16), ("dp", "row")).astype(jnp.float32),
         lax.psum(res_bias_grad.astype(jnp.bfloat16), ("dp", "row")).astype(jnp.float32),
         lax.psum(gain_grad.astype(jnp.bfloat16), ("dp", "row")).astype(jnp.float32),

time: 1060 us -> 1060 us (level)
  blocking collectives: 25.2 us -> 40 us
  waiting for transfers between devices: 744 us -> 730 us
    all_gather x1, waiting for transfers between devices: 17.9 us -> 2.64 us  [per_device(): lax.all_gather(pieces_now[2].astype(jnp.bfloat16), 'dp', axis=1, tiled=True)]
    all_gather x0 -> x1, blocking collectives: none -> 14.8 us  [per_device(): lax.all_gather(qkv_bias_grad.astype(jnp.bfloat16), ('dp', 'row'))]
where the time goes in v1:
time: 1060 us
  waiting for transfers between devices  730 us (69%)
  matrix products  128 us (12%)
  local copies, waits for them, and re-layouts  74.6 us (7%)
  other arithmetic  67.2 us (6%)
  blocking collectives  40 us (4%)
  between operations  15 us (1%)
    all_gather x1, waiting for transfers between devices, per_device(): lax.all_gather(w_down.astype(jnp.bfloat16), 'row', axis=1, tiled=True)  96.3 us
    all_gather x1, waiting for transfers between devices, per_device(): lax.all_gather(w_qkv.astype(jnp.bfloat16), 'row', axis=0, tiled=True)  76.9 us
    reduce_scatter x1, waiting for transfers between devices, per_device(): lax.psum_scatter(reorder_cols(down_grad, row_count, dp_count).astype(jnp....  75.3 us
    all_gather x1, waiting for transfers between devices, per_device(): lax.all_gather(w_up.astype(jnp.bfloat16), 'row', axis=0, tiled=True)  65.6 us
    reduce_scatter x1, waiting for transfers between devices, per_device(): lax.psum_scatter(reorder_rows(qkv_weight_grad, row_count, dp_count).astyp...  65.5 us
    reduce_scatter x1, waiting for transfers between devices, per_device(): lax.psum_scatter(reorder_rows(up_weight_grad, row_count, dp_count).astype...  63.2 us
    all_gather x1, waiting for transfers between devices, per_device(): grad_full = lax.all_gather(cotangent, 'col', axis=1, tiled=True)  47.1 us
    reduce_scatter x1, waiting for transfers between devices, per_device(): lax.psum_scatter(branch_terms.astype(jnp.bfloat16), 'col', scatter_dimens...  43.2 us
  transfers between devices with their start and end apart: 19, of which 19 were waited for; matrix products, arithmetic and copies ran while one was open for 23% of the time, Pallas kernels for 0%

profile of v1, /device:TPU:0, one launch (start us, length us, event | category | flops | bytes accessed | tf_op | source)
XLA Modules:
  0.0 1055.1 jit_solution(9910991833248770281)
XLA Ops:
  16.1 41.9 %all-gather.14.cloned.1.call-done = bf16[512,2048]{1,0:T(8,128)(2,1)} async-done(((bf16[512,512]{1,0:T(8,128)(2,1)}), bf16[512,2048]{1,0:T(8,128)(2,1)}) %all-gather.14.cloned.1.call-update) | async-done | bytes 2097168 | tf_op jit(solution)/shard_map/all_gather | solution.py:108
  62.4 76.9 %all-gather.16.cloned.1.call-done = bf16[2048,1536]{1,0:T(8,128)(2,1)} async-done(((bf16[1024,1536]{1,0:T(8,128)(2,1)}), bf16[2048,1536]{1,0:T(8,128)(2,1)}) %all-gather.16.cloned.1.call-update) | async-done | bytes 6291472 | tf_op jit(solution)/shard_map/all_gather | solution.py:114
  174.5 47.1 %all-gather.28.cloned.1.call-done = bf16[512,2048]{1,0:T(8,128)(2,1)} async-done(((bf16[512,512]{1,0:T(8,128)(2,1)}), bf16[512,2048]{1,0:T(8,128)(2,1)}) %all-gather.28.cloned.1.call-update) | async-done | bytes 2097168 | tf_op jit(solution)/shard_map/all_gather | solution.py:177
  227.0 16.7 %all-gather.18.cloned.1.call-done = bf16[1024,512]{0,1:T(8,128)(2,1)} async-done(((bf16[512,512]{0,1:T(8,128)(2,1)}), bf16[1024,512]{0,1:T(8,128)(2,1)}) %all-gather.18.cloned.1.call-update) | async-done | bytes 1048592 | tf_op jit(solution)/shard_map/all_gather | solution.py:142
  254.9 12.1 %all-gather.20.cloned.1.call-done = bf16[1024,512]{0,1:T(8,128)(2,1)} async-done(((bf16[512,512]{0,1:T(8,128)(2,1)}), bf16[1024,512]{0,1:T(8,128)(2,1)}) %all-gather.20.cloned.1.call-update) | async-done | bytes 1048592 | tf_op jit(solution)/shard_map/all_gather | solution.py:143
  280.0 9.9 multiply_convert_fusion
  307.6 65.6 %all-gather.24.cloned.1.call-done = bf16[2048,2048]{1,0:T(8,128)(2,1)} async-done(((bf16[1024,2048]{1,0:T(8,128)(2,1)}), bf16[2048,2048]{1,0:T(8,128)(2,1)}) %all-gather.24.cloned.1.call-update) | async-done | bytes 8388624 | tf_op jit(solution)/shard_map/all_gather | solution.py:115
  373.2 9.8 fusion.64
  383.0 96.3 %all-gather.26.cloned.1.call-done = bf16[2048,2048]{1,0:T(8,128)(2,1)} async-done(((bf16[2048,1024]{1,0:T(8,128)(2,1)}), bf16[2048,2048]{1,0:T(8,128)(2,1)}) %all-gather.26.cloned.1.call-update) | async-done | bytes 8388624 | tf_op jit(solution)/shard_map/all_gather | solution.py:117
  479.3 13.4 %fusion.65 = (bf16[2048]{0:T(1024)(128)(2,1)S(1)}, bf16[512,2048]{1,0:T(8,128)(2,1)}) fusion(f32[512,2048]{1,0:T(8,128)} %fusion.64, f32[2048]{0:T(1024)S(1)} %copy-done.29, bf16[512,2048]{1,0:T(8,128)(2,1)} %all-gather.28.cloned.1.call-done, bf16[2048,2048]{1,0:T(8,128)(2,1)} %all-gather.26.cloned.1.call-done), kind=kOutput, calls=%fused_computation.132 | convolution fusion | flops 4318033920 | bytes 16789504 | tf_op jit(solution)/shard_map/td,fd->tf/dot_general | solution.py:181
  492.7 21.3 %reduce-scatter.9.cloned.1.call-done = bf16[512,1024]{0,1:T(8,128)(2,1)} async-done(((bf16[1024,1024]{0,1:T(8,128)(2,1)}), bf16[512,1024]{0,1:T(8,128)(2,1)}) %reduce-scatter.9.cloned.1.call-update) | async-done | bytes 1048592 | tf_op jit(solution)/shard_map/reduce_scatter | solution.py:221
  556.4 11.0 %convolution_convert_fusion = bf16[2048,2048]{0,1:T(8,128)(2,1)} fusion(bf16[512,2048]{1,0:T(8,128)(2,1)} %all-gather.28.cloned.1.call-done, f32[512,2048]{1,0:T(8,128)} %fusion.64, f32[2048]{0:T(1024)S(1)} %copy-done.29), kind=kOutput, calls=%fused_computation.21 | convolution fusion | flops 4309647360 | bytes 14688256 | tf_op jit(solution)/shard_map/tf,td->fd/dot_general | solution.py:179
  567.4 21.7 %copy.57 = bf16[2048,4,2,256]{3,2,1,0:T(2,128)(2,1)} copy(bf16[2048,4,2,256]{0,3,1,2:T(8,128)(2,1)} %bitcast.110) | data formatting | bytes 16777216 | tf_op jit(solution)/shard_map/convert_element_type | solution.py:279
  589.2 14.4 %convert_element_type.257 = bf16[2048,2048]{1,0:T(8,128)(2,1)} reshape(bf16[2048,4,2,256]{3,2,1,0:T(2,128)(2,1)} %copy.57) | data formatting | bytes 16777216 | tf_op jit(solution)/shard_map/convert_element_type | solution.py:279
  603.7 13.0 %all-reduce.9.cloned.1.call-done = bf16[512,2048]{1,0:T(8,128)(2,1)} async-done(((bf16[512,2048]{1,0:T(8,128)(2,1)}), bf16[512,2048]{1,0:T(8,128)(2,1)}) %all-reduce.9.cloned.1.call-update) | async-done | bytes 2097168 | tf_op jit(solution)/shard_map/psum | solution.py:238
  634.6 25.6 %reduce-scatter.13.cloned.1.call-done = bf16[512,256]{0,1:T(8,128)(2,1)} async-done(((bf16[512,2048]{0,1:T(8,128)(2,1)}), bf16[512,256]{0,1:T(8,128)(2,1)}) %reduce-scatter.13.cloned.1.call-update) | async-done | bytes 262160 | tf_op jit(solution)/shard_map/reduce_scatter | solution.py:272
  672.4 63.2 %reduce-scatter.15.cloned.1.call-done = bf16[256,2048]{1,0:T(8,128)(2,1)} async-done(((bf16[2048,2048]{1,0:T(8,128)(2,1)}), bf16[256,2048]{1,0:T(8,128)(2,1)}) %reduce-scatter.15.cloned.1.call-update) | async-done | bytes 1048592 | tf_op jit(solution)/shard_map/reduce_scatter | solution.py:266
  735.7 75.3 %reduce-scatter.17.cloned.1.call-done = bf16[2048,256]{1,0:T(8,128)(2,1)} async-done(((bf16[2048,2048]{1,0:T(8,128)(2,1)}), bf16[2048,256]{1,0:T(8,128)(2,1)}) %reduce-scatter.17.cloned.1.call-update) | async-done | bytes 1048592 | tf_op jit(solution)/shard_map/reduce_scatter | solution.py:278
  811.1 65.5 %reduce-scatter.11.cloned.1.call-done = bf16[256,1536]{1,0:T(8,128)(2,1)} async-done(((bf16[2048,1536]{1,0:T(8,128)(2,1)}), bf16[256,1536]{1,0:T(8,128)(2,1)}) %reduce-scatter.11.cloned.1.call-update) | async-done | bytes 786448 | tf_op jit(solution)/shard_map/reduce_scatter | solution.py:260
  876.8 14.8 %all-gather = bf16[8,1,1536]{2,1,0:T(2,128)(2,1)S(1)} all-gather(bf16[1,1,1536]{2,1,0:T(2,128)(2,1)S(1)} %reshape.249), channel_id=1, replica_groups=mesh['dp'=4,'row'=2,'col'=4] {'dp','row'}, dimensions={0}, use_global_device_ids=true | all-gather | bytes 27648 | tf_op jit(solution)/shard_map/all_gather | solution.py:251
  897.5 43.2 %reduce-scatter.7.cloned.1.call-done = bf16[512,512]{1,0:T(8,128)(2,1)} async-done(((bf16[512,2048]{1,0:T(8,128)(2,1)}), bf16[512,512]{1,0:T(8,128)(2,1)}) %reduce-scatter.7.cloned.1.call-update) | async-done | bytes 524304 | tf_op jit(solution)/shard_map/reduce_scatter | solution.py:173
  943.1 25.2 %all-reduce.6 = (bf16[2048]{0:T(1024)(128)(2,1)S(1)}, bf16[512]{0:T(512)(128)(2,1)S(1)}, bf16[2048]{0:T(1024)(128)(2,1)S(1)}, bf16[2048]{0:T(1024)(128)(2,1)S(1)}) all-reduce(bf16[2048]{0:T(1024)(128)(2,1)S(1)} %get-tuple-element.79, bf16[512]{0:T(512)(128)(2,1)S(1)} %reduce_sum.122, ...), channel_id=1, replica_groups=mesh['dp'=4,'row'=2,'col'=4] {'dp','row'}, use_global_device_ids=true, to_apply=%region_17.18 | all-reduce | flops 6656 | bytes 26624 | tf_op jit(solution)/shard_map/psum | solution.py:254
  982.7 29.9 %all-gather.36.cloned.1.call-done = bf16[2048,1024]{1,0:T(8,128)(2,1)} async-done(((bf16[2048,256]{1,0:T(8,128)(2,1)}), bf16[2048,1024]{1,0:T(8,128)(2,1)}) %all-gather.36.cloned.1.call-update) | async-done | bytes 4194320 | tf_op jit(solution)/shard_map/all_gather | solution.py:295
  1019.1 23.5 %all-gather.30.cloned.1.call-done = bf16[1024,1536]{1,0:T(8,128)(2,1)} async-done(((bf16[256,1536]{1,0:T(8,128)(2,1)}), bf16[1024,1536]{1,0:T(8,128)(2,1)}) %all-gather.30.cloned.1.call-update) | async-done | bytes 3145744 | tf_op jit(solution)/shard_map/all_gather | solution.py:286
  (201 shorter events, 203.3 us)
Async XLA Ops:
  7.2 50.8 %all-gather.14.cloned.1.call-start = ((), (), s32[]{:S(2)}) async-start(), calls=%async_computation.6 | async-start | bytes 2621440 | tf_op jit(solution)/shard_map/all_gather | solution.py:108
  7.9 131.4 %all-gather.16.cloned.1.call-start = ((), (), s32[]{:S(2)}) async-start(), calls=%async_computation.7 | async-start | bytes 9437184 | tf_op jit(solution)/shard_map/all_gather | solution.py:114
  13.0 161.5 %all-gather.22.cloned.1.call-start = ((), (), s32[]{:S(2)}) async-start(), calls=%async_computation.10 | async-start | bytes 3145728 | tf_op jit(solution)/shard_map/all_gather | solution.py:116
  14.2 207.4 %all-gather.28.cloned.1.call-start = ((), (), s32[]{:S(2)}) async-start(), calls=%async_computation.14 | async-start | bytes 2621440 | tf_op jit(solution)/shard_map/all_gather | solution.py:177
  14.8 228.9 %all-gather.18.cloned.1.call-start = ((), (), s32[]{:S(2)}) async-start(), calls=%async_computation.8 | async-start | bytes 1572864 | tf_op jit(solution)/shard_map/all_gather | solution.py:142
  152.2 114.9 %all-gather.20.cloned.1.call-start = ((), (), s32[]{:S(2)}) async-start(), calls=%async_computation.9 | async-start | bytes 1572864 | tf_op jit(solution)/shard_map/all_gather | solution.py:143
  153.1 220.1 %all-gather.24.cloned.1.call-start = ((), (), s32[]{:S(2)}) async-start(), calls=%async_computation.11 | async-start | bytes 12582912 | tf_op jit(solution)/shard_map/all_gather | solution.py:115
  159.2 320.1 %all-gather.26.cloned.1.call-start = ((), (), s32[]{:S(2)}) async-start(), calls=%async_computation.12 | async-start | bytes 12582912 | tf_op jit(solution)/shard_map/all_gather | solution.py:117
  165.4 348.7 %reduce-scatter.9.cloned.1.call-start = ((), (), s32[]{:S(2)}) async-start(), calls=%async_computation.15 | async-start | bytes 3145728 | tf_op jit(solution)/shard_map/reduce_scatter | solution.py:221
  300.2 316.5 %all-reduce.9.cloned.1.call-start = ((), (), s32[]{:S(2)}) async-start(), calls=%async_computation.16 | async-start | bytes 4194304 | tf_op jit(solution)/shard_map/psum | solution.py:238
  307.6 171.7 %copy-start.29 = (f32[2048]{0:T(1024)S(1)}, f32[2048]{0:T(1024)}, u32[]{:S(2)}) copy-start(f32[2048]{0:T(1024)} %param.22) | copy-start | bytes 24580
  530.4 129.8 %reduce-scatter.13.cloned.1.call-start = ((), (), s32[]{:S(2)}) async-start(), calls=%async_computation.19 | async-start | bytes 2359296 | tf_op jit(solution)/shard_map/reduce_scatter | solution.py:272
  539.0 196.6 %reduce-scatter.15.cloned.1.call-start = ((), (), s32[]{:S(2)}) async-start(), calls=%async_computation.21 | async-start | bytes 9437184 | tf_op jit(solution)/shard_map/reduce_scatter | solution.py:266
  556.4 254.6 %reduce-scatter.17.cloned.1.call-start = ((), (), s32[]{:S(2)}) async-start(), calls=%async_computation.23 | async-start | bytes 9437184 | tf_op jit(solution)/shard_map/reduce_scatter | solution.py:278
  603.6 272.9 %reduce-scatter.11.cloned.1.call-start = ((), (), s32[]{:S(2)}) async-start(), calls=%async_computation.17 | async-start | bytes 7077888 | tf_op jit(solution)/shard_map/reduce_scatter | solution.py:260
  634.5 260.4 %all-gather.32.cloned.1.call-start = ((), (), s32[]{:S(2)}) async-start(), calls=%async_computation.20 | async-start | bytes 1310720 | tf_op jit(solution)/shard_map/all_gather | solution.py:292
  660.2 280.5 %reduce-scatter.7.cloned.1.call-start = ((), (), s32[]{:S(2)}) async-start(), calls=%async_computation.13 | async-start | bytes 2621440 | tf_op jit(solution)/shard_map/reduce_scatter | solution.py:173
  672.3 204.3 %copy-start.5 = (bf16[512,512]{1,0:T(8,128)(2,1)S(1)}, bf16[512,512]{1,0:T(8,128)(2,1)}, u32[]{:S(2)}) copy-start(bf16[512,512]{1,0:T(8,128)(2,1)} %param.27) | copy-start | bytes 1572868
  672.3 268.5 %copy-start.8 = (bf16[512,512]{1,0:T(8,128)(2,1)S(1)}, bf16[512,512]{1,0:T(8,128)(2,1)}, u32[]{:S(2)}) copy-start(bf16[512,512]{1,0:T(8,128)(2,1)} %param.15) | copy-start | bytes 1572868
  672.3 268.5 %copy-start.27 = (f32[512]{0:T(512)S(1)}, f32[512]{0:T(512)}, u32[]{:S(2)}) copy-start(f32[512]{0:T(512)} %param.24) | copy-start | bytes 6148
  672.3 270.4 %copy-start.4 = (bf16[512,2048]{1,0:T(8,128)(2,1)S(1)}, bf16[512,2048]{1,0:T(8,128)(2,1)}, u32[]{:S(2)}) copy-start(bf16[512,2048]{1,0:T(8,128)(2,1)} %all-reduce.9.cloned.1.call-done) | copy-start | bytes 6291460
  672.3 303.7 %all-gather.34.cloned.1.call-start = ((), (), s32[]{:S(2)}) async-start(), calls=%async_computation.22 | async-start | bytes 5242880 | tf_op jit(solution)/shard_map/all_gather | solution.py:289
  735.6 276.9 %all-gather.36.cloned.1.call-start = ((), (), s32[]{:S(2)}) async-start(), calls=%async_computation.24 | async-start | bytes 5242880 | tf_op jit(solution)/shard_map/all_gather | solution.py:295
  811.0 231.6 %all-gather.30.cloned.1.call-start = ((), (), s32[]{:S(2)}) async-start(), calls=%async_computation.18 | async-start | bytes 3932160 | tf_op jit(solution)/shard_map/all_gather | solution.py:286
  (31 other events, 839.1 us)
Sparse Core Ops, SparseCore 0:
  9.6 48.3 all-gather.13
  60.1 79.1 all-gather.15
  141.4 33.0 all-gather.21
  176.0 45.6 all-gather.27
  223.6 20.0 all-gather.17
  245.7 21.2 all-gather.19
  269.1 104.0 all-gather.23
  375.3 103.9 all-gather.25
  482.1 31.8 reduce-scatter.8
  530.5 86.1 all-reduce.8
  620.0 40.1 reduce-scatter.12
  664.1 71.5 reduce-scatter.14
  739.6 71.2 reduce-scatter.16
  814.8 61.7 reduce-scatter.10
  878.0 16.8 all-gather.31
  897.1 43.6 reduce-scatter.6
  942.2 33.8 all-gather.33
  977.4 35.0 all-gather.35
  1014.1 28.4 all-gather.29
